TPU v7x, 128 devices: a whole 4x4x4 slice. The times are simulated.
128 devices in a mesh: seq: 4 (over z), head: 32 (over x, y, core).
Axes of the slice: x: 4, y: 4, z: 4, core: 2. Of those that a mesh axis runs over, the one named last changes fastest.
Arguments:
- inputs: bfloat16 [2048, 8192], P('seq'), may hold values from -6 to 6
- w_qkv: bfloat16 [3, 8192, 8192], P(None, None, 'head'), may hold values from -0.0625 to 0.0625
- w_out: bfloat16 [8192, 8192], P('head'), may hold values from -0.125 to 0.125
- turn_ids: int32 [4, 512], P('seq'), may hold values from 0 to 15, never falling along the last dimension, each value on 1 to 64 neighbouring positions
- picked: int32 [4, 64], P('seq'), may hold values from 0 to 511
- owners: int32 [256, 1], P('seq'), may hold values from 0 to 31; in each aligned block of 64 rows (0 to 63, 64 to 127, ...) at most 8 rows name the same one
- candidates: bfloat16 [8192, 8192], P(('seq', 'head')), may hold values from -0.25 to 0.25
Outputs:
- mixed: bfloat16 [2048, 8192], P('seq', 'head')
- scores: float32 [1024, 64], P(('seq', 'head'))
Inputs may be any that keep to these rules, and one draw needn't show every extreme that they name: `turn_ids`: within each session turn numbers start at 0, never fall, and each turn has 1 to 64 tokens. `owners`: among the 64 picked rows of one session no owner is named more than 8 times.
All inputs are finite; a program needn't handle non-finite values.
Results may differ from a plain program's by a relative error of at most 0.008.
Values may be sent and summed in bfloat16 or wider, within the bound.
A program may use at most 128 MiB of HBM per device.

v0:
```python
import jax
import jax.numpy as jnp
from jax import lax
from jax.sharding import PartitionSpec as P

HDIM = 128


def carried_in(value, axis, join, neutral):
    count, mine = (lax.axis_size(axis), lax.axis_index(axis))
    pieces = lax.all_gather(value, axis)
    so_far = jnp.full_like(value, 0) + jnp.asarray(neutral, value.dtype)

    def lap(position, so_far):
        longer = join(so_far, pieces[position])
        return jnp.where(position < mine, longer, so_far)

    return lax.fori_loop(0, count - 1, lap, so_far)


def per_device(inputs, w_qkv, w_out, turn_ids, picked, owners, candidates):
    tokens_here = inputs.shape[0]
    model_width = inputs.shape[1]
    heads_here = w_qkv.shape[2] // HDIM
    n_head = lax.axis_size("head")
    col_count = model_width // n_head
    projected = lax.dot_general(
        inputs, w_qkv, (((1,), (1,)), ((), ())), preferred_element_type=jnp.float32
    ).astype(jnp.bfloat16)
    query = projected[:, 0].reshape(tokens_here, heads_here, HDIM)
    keys = projected[:, 1].reshape(tokens_here, heads_here, HDIM)
    values = projected[:, 2].reshape(tokens_here, heads_here, HDIM)
    states = jnp.einsum("thi,thj->hij", keys, values, preferred_element_type=jnp.float32)
    prefix = carried_in(states, "seq", jnp.add, jnp.zeros_like(states))
    prefix = prefix.astype(jnp.bfloat16)
    scores_local = jnp.einsum("thi,shi->hts", query, keys, preferred_element_type=jnp.float32)
    tok_pos = jnp.arange(tokens_here, dtype=jnp.int32)
    causal = tok_pos[:, None] >= tok_pos[None, :]
    weights = jnp.where(causal[None, :, :], scores_local, 0.0).astype(jnp.bfloat16)
    local_part = jnp.einsum("hts,shj->thj", weights, values, preferred_element_type=jnp.float32)
    carried = jnp.einsum("thi,hij->thj", query, prefix, preferred_element_type=jnp.float32)
    summed = local_part + carried
    normed = summed * lax.rsqrt(jnp.mean(summed * summed, axis=-1, keepdims=True) + 1e-05)
    attended = normed.astype(jnp.bfloat16).reshape(tokens_here, heads_here * HDIM)
    input_cols = lax.dynamic_slice_in_dim(inputs, lax.axis_index("head") * col_count, col_count, 1)
    branch = lax.psum_scatter(
        lax.dot_general(
            w_out, attended, (((0,), (1,)), ((), ())), preferred_element_type=jnp.float32
        ),
        "head",
        scatter_dimension=0,
        tiled=True,
    ).T
    mixed = (input_cols.astype(jnp.float32) + branch).astype(jnp.bfloat16)
    turn_row = turn_ids[0]
    pick_row = picked[0]
    r_dev = pick_row.shape[0]
    cap_rows = 4 * r_dev // n_head
    pick_hot = tok_pos[None, :] == pick_row[:, None]
    sel_turn = jnp.sum(jnp.where(pick_hot, turn_row[None, :], 0), axis=1)
    member = (turn_row[None, :] == sel_turn[:, None]) & (tok_pos[None, :] <= pick_row[:, None])
    row_count = jnp.sum(member.astype(jnp.float32), axis=1)
    pooled = jnp.dot(member.astype(jnp.bfloat16), mixed, preferred_element_type=jnp.float32)
    summary = (pooled / row_count[:, None]).astype(jnp.bfloat16)
    owner_row = owners[:, 0]
    row_pos = jnp.arange(r_dev, dtype=jnp.int32)
    head_pos = jnp.arange(n_head, dtype=jnp.int32)
    own_hot = (owner_row[:, None] == head_pos[None, :]).astype(jnp.int32)
    before = (row_pos[:, None] > row_pos[None, :]).astype(jnp.int32)
    slot_rank = jnp.sum(jnp.dot(before, own_hot) * own_hot, axis=1)
    slot_index = owner_row * cap_rows + slot_rank
    dispatch = (
        slot_index[None, :] == jnp.arange(n_head * cap_rows, dtype=jnp.int32)[:, None]
    ).astype(jnp.bfloat16)
    outgoing = jnp.dot(dispatch, summary, preferred_element_type=jnp.float32).astype(jnp.bfloat16)
    outgoing = outgoing.reshape(n_head, cap_rows, col_count)
    cand_parts = candidates.reshape(candidates.shape[0], n_head, col_count)
    scores = jnp.einsum(
        "skc,nsc->kn",
        lax.all_to_all(outgoing, "head", split_axis=0, concat_axis=0, tiled=True),
        cand_parts,
        preferred_element_type=jnp.float32,
    )
    return (mixed, scores)


def solution(mesh):
    return jax.shard_map(
        per_device,
        mesh=mesh,
        in_specs=(
            P("seq", None),
            P(None, None, "head"),
            P("head", None),
            P("seq", None),
            P("seq", None),
            P("seq", None),
            P(("seq", "head"), None),
        ),
        out_specs=(P("seq", "head"), P(("seq", "head"), None)),
        check_vma=False,
    )
```

profile of v0, /device:TPU:1, one launch (start us, length us, event | category | flops | bytes accessed | tf_op | source)
XLA Modules:
  0.0 185.9 jit_solution(2698635820997806817)
XLA Ops:
  7.2 0.0 reduce-scatter.2.cloned.1.call-start
  7.2 0.1 iota_compare_fusion
  7.3 12.2 %fusion.2 = bf16[512,3,256]{0,2,1:T(8,128)(2,1)S(1)} fusion(bf16[3,8192,256]{2,1,0:T(8,128)(2,1)} %param.10, bf16[512,8192]{1,0:T(8,128)(2,1)} %param.9), kind=kOutput, calls=%fused_computation.5 | convolution fusion | flops 6442844160 | bytes 21757952 | tf_op jit(solution)/shard_map/dot_general | solution.py:27
  19.5 0.1 fusion.31
  19.5 0.2 fusion.32
  19.8 13.4 %all-gather = f32[8,128,128]{2,1,0:T(8,128)S(1)} all-gather(f32[2,128,128]{2,1,0:T(8,128)S(1)} %fusion.32), channel_id=2, replica_groups=mesh['seq'=4,'head'=32] {'seq'}, dimensions={0}, use_global_device_ids=true | all-gather | bytes 655360 | tf_op jit(solution)/shard_map/all_gather | solution.py:11
  33.1 0.2 while.14
  33.3 0.3 fusion.24
  33.6 0.8 multiply_reduce_fusion
  34.4 0.1 multiply_convert_fusion
  34.5 10.3 %convolution_bitcast_fusion = f32[8192,512]{0,1:T(8,128)} fusion(bf16[512,256]{0,1:T(8,128)(2,1)S(1)} %bitcast.53, bf16[256,8192]{1,0:T(8,128)(2,1)} %param.11), kind=kOutput, calls=%fused_computation.1 | convolution fusion | flops 2147483648 | bytes 21233664 | tf_op jit(solution)/shard_map/dot_general | solution.py:47
  44.8 0.0 reduce-scatter.2.cloned.1.call-update
  44.8 0.6 copy-done.4
  45.4 0.1 fusion.10
  45.6 0.0 copy-done.2
  45.6 0.2 select_reduce_fusion
  45.8 0.2 convert_reduce_fusion
  46.0 115.9 %reduce-scatter.2.cloned.1.call-done = f32[256,512]{0,1:T(8,128)} async-done(((f32[8192,512]{0,1:T(8,128)}), f32[256,512]{0,1:T(8,128)}) %reduce-scatter.2.cloned.1.call-update) | async-done | bytes 524304 | tf_op jit(solution)/shard_map/reduce_scatter | solution.py:46
  161.8 1.2 fusion.15
  163.0 0.0 copy-start.1
  163.0 0.4 fusion.8
  163.5 14.6 %all_to_all.5 = bf16[32,8,256]{2,1,0:T(8,128)(2,1)S(1)} all-to-all(bf16[32,8,256]{2,1,0:T(8,128)(2,1)S(1)} %fusion.8), channel_id=1, replica_groups=mesh['seq'=4,'head'=32] {'head'}, dimensions={0} | all-to-all | bytes 262144 | tf_op jit(solution)/shard_map/all_to_all | solution.py:80
  178.0 0.0 copy-done
  178.0 1.0 convolution_bitcast_fusion.1
  (12 shorter events, 0.1 us)
Async XLA Ops:
  7.2 154.7 %reduce-scatter.2.cloned.1.call-start = ((), (), s32[]{:S(2)}) async-start(), calls=%async_computation.2 | async-start | bytes 17301504 | tf_op jit(solution)/shard_map/reduce_scatter | solution.py:46
  44.8 0.7 copy-start.4
  44.8 0.8 copy-start.2
  44.8 0.8 copy-start.3
  44.8 133.3 %copy-start = (bf16[64,8192]{1,0:T(8,128)(2,1)S(1)}, bf16[64,8192]{1,0:T(8,128)(2,1)}, u32[]{:S(2)}) copy-start(bf16[64,8192]{1,0:T(8,128)(2,1)} %param.15) | copy-start | bytes 3145732
  163.0 16.0 %copy-start.1 = (bf16[512,256]{1,0:T(8,128)(2,1)}, bf16[512,256]{1,0:T(8,128)(2,1)S(1)}, u32[]{:S(2)}) copy-start(bf16[512,256]{1,0:T(8,128)(2,1)S(1)} %fusion.15) | copy-start | bytes 786436
Sparse Core Ops, SparseCore 0:
  44.9 116.8 reduce-scatter.1
where the time goes:
time: 186 us
  waiting for transfers between devices  116 us (62%)
  blocking collectives  28 us (15%)
  matrix products  25.3 us (14%)
  between operations  14.2 us (8%)
    reduce_scatter x1, waiting for transfers between devices, per_device(): lax.psum_scatter(lax.dot_general(w_out, attended, (((0,), (1,)), ((), ())...  116 us
    all_to_all x1, blocking collectives, per_device(): lax.all_to_all(outgoing, 'head', split_axis=0, concat_axis=0, tiled=True)  14.6 us
    all_gather x1, blocking collectives, carried_in(): pieces = lax.all_gather(value, axis)  13.4 us
    dot_general x1, matrix products, per_device(): lax.dot_general(inputs, w_qkv, (((1,), (1,)), ((), ())), preferred_elemen...  12.2 us
    dot_general x1, matrix products, per_device(): lax.dot_general(w_out, attended, (((0,), (1,)), ((), ())), preferred_elem...  10.3 us
  transfers between devices with their start and end apart: 1, of which 1 were waited for; matrix products, arithmetic and copies ran while one was open for 0% of the time, Pallas kernels for 0%

commit v1 on v0

v1 whole, which is shorter than its diff:
```python
import functools

import jax
import jax.numpy as jnp
from jax import lax
from jax.experimental import pallas as pl
from jax.experimental.pallas import tpu as pltpu
from jax.sharding import PartitionSpec as P

HDIM = 128
SIDE = 4
KB = 1024
AHEAD = 4
NQ = 2
MESH = pl.DeviceIdType.MESH
BF = jnp.bfloat16
F32 = jnp.float32


def mm(a, b, dims=((1,), (0,))):
    return lax.dot_general(a, b, (dims, ((), ())), preferred_element_type=F32)


def kernel(
    x_hbm, wqkv_hbm, wout_hbm, turn_ref, picked_ref, owners_ref, cand_hbm,
    mixed_ref, scores_ref,
    xbuf, wbuf, acc, qkv, st, st_in, pre, a2, w2, c, r1, s1, r2, xcols, outb, inb, cand,
    xsem, wsem, msem, w2l, w2s, w2r, sts, strr, a2s, a2r, s1s, s1r, s2s, s2r, aas, aar,
):
    tokens, col = xcols.shape
    nk = xbuf.shape[0]
    n_head = outb.shape[0]
    n_seq = st_in.shape[0] + 1
    half = tokens // 2
    piece = half // NQ
    hp = piece // 2
    z = lax.axis_index("seq")
    me = lax.axis_index("head")
    core = lax.rem(me, 2)
    cy = lax.rem(lax.div(me, 2), SIDE)
    cx = lax.div(me, 2 * SIDE)

    def at(px, py, pc):
        return (px * SIDE + py) * 2 + pc

    sib = at(cx, cy, 1 - core)

    def x_load(k):
        return pltpu.make_async_copy(
            x_hbm.at[:, pl.ds(pl.multiple_of(k * KB, KB), KB)], xbuf.at[k], xsem.at[k]
        )

    def w_load(n, k):
        return pltpu.make_async_copy(
            wqkv_hbm.at[n, pl.ds(pl.multiple_of(k * KB, KB), KB), :], wbuf.at[n, k], wsem.at[n, k]
        )

    def remote(src, dst, ssem, rsem, to):
        return pltpu.make_async_remote_copy(
            src_ref=src, dst_ref=dst, send_sem=ssem, recv_sem=rsem, device_id=to, device_id_type=MESH
        )

    for k in range(AHEAD):
        x_load(k).start()
        w_load(1, k).start()
        w_load(2, k).start()

    barrier = pltpu.get_barrier_semaphore()

    def greet(i, carry):
        pl.semaphore_signal(
            barrier, inc=1, device_id={"head": lax.rem(me + i, n_head)}, device_id_type=MESH
        )
        return carry

    lax.fori_loop(1, n_head, greet, 0)
    for d in range(1, n_seq):
        pl.semaphore_signal(
            barrier, inc=1, device_id={"seq": lax.rem(z + d, n_seq)}, device_id_type=MESH
        )

    acc[...] = jnp.zeros_like(acc)

    def kv_step(k, carry):
        x_load(k).wait()
        w_load(1, k).wait()
        w_load(2, k).wait()

        @pl.when(k + AHEAD < nk)
        def _():
            x_load(k + AHEAD).start()
            w_load(1, k + AHEAD).start()
            w_load(2, k + AHEAD).start()

        @pl.when(k + AHEAD >= nk)
        def _():
            w_load(0, k + AHEAD - nk).start()

        acc[1] += mm(xbuf[k], wbuf[1, k])
        acc[2] += mm(xbuf[k], wbuf[2, k])
        return carry

    lax.fori_loop(0, nk, kv_step, 0)
    qkv[1] = acc[1].astype(BF)
    qkv[2] = acc[2].astype(BF)

    pl.semaphore_wait(barrier, n_head - 1 + n_seq - 1)

    for h in range(2):
        hs = slice(h * HDIM, (h + 1) * HDIM)
        st[h] = mm(qkv[1, :, hs], qkv[2, :, hs], ((0,), (0,))).astype(BF)
    state_copies = [
        remote(st, st_in.at[d - 1], sts.at[d - 1], strr.at[d - 1], {"seq": lax.rem(z + d, n_seq)})
        for d in range(1, n_seq)
    ]
    for cp in state_copies:
        cp.start()

    w2_local, w2_remote = [], []
    for j in range(SIDE * SIDE):
        jx, jy = j // SIDE, j % SIDE
        mine = pl.ds(pl.multiple_of((2 * j + core) * col, col), col)
        theirs = pl.ds(pl.multiple_of((2 * j + 1 - core) * col, col), col)
        w2_local.append(
            pltpu.make_async_copy(wout_hbm.at[:, mine], w2.at[jx, jy, core], w2l.at[j])
        )
        w2_remote.append(
            remote(wout_hbm.at[:, theirs], w2.at[jx, jy, core], w2s.at[j], w2r.at[j], {"head": sib})
        )
    for cp in w2_local + w2_remote:
        cp.start()
    x_cols = pltpu.make_async_copy(
        x_hbm.at[:, pl.ds(pl.multiple_of(me * col, col), col)], xcols, msem.at[0]
    )
    x_cols.start()
    cand_load = pltpu.make_async_copy(cand_hbm, cand, msem.at[1])
    cand_load.start()

    def q_step(k, carry):
        w_load(0, k).wait()

        @pl.when(k + AHEAD < nk)
        def _():
            w_load(0, k + AHEAD).start()

        acc[0] += mm(xbuf[k], wbuf[0, k])
        return carry

    lax.fori_loop(0, nk, q_step, 0)
    qkv[0] = acc[0].astype(BF)

    for b in range(2):
        rows = slice(b * half, (b + 1) * half)
        seen = (b + 1) * half
        ok = (
            lax.broadcasted_iota(jnp.int32, (half, seen), 0) + b * half
            >= lax.broadcasted_iota(jnp.int32, (half, seen), 1)
        )
        for h in range(2):
            hs = slice(h * HDIM, (h + 1) * HDIM)
            sc = mm(qkv[0, rows, hs], qkv[1, :seen, hs], ((1,), (1,)))
            sc = jnp.where(ok, sc, 0.0).astype(BF)
            pre[rows, hs] = mm(sc, qkv[2, :seen, hs])

    for cp in state_copies:
        cp.wait_recv()
    prefix = []
    for h in range(2):
        total = jnp.zeros((HDIM, HDIM), F32)
        for d in range(1, n_seq):
            total = total + jnp.where(z >= d, st_in[d - 1, h].astype(F32), 0.0)
        prefix.append(total.astype(BF))
    a2_copies = []
    for b in range(2):
        rows = slice(b * half, (b + 1) * half)
        for h in range(2):
            hs = slice(h * HDIM, (h + 1) * HDIM)
            summed = pre[rows, hs] + mm(qkv[0, rows, hs], prefix[h])
            normed = summed * lax.rsqrt(jnp.mean(summed * summed, axis=-1, keepdims=True) + 1e-05)
            a2[core, rows, hs] = normed.astype(BF)
        cp = remote(a2.at[core, rows], a2.at[core, rows], a2s.at[b], a2r.at[b], {"head": sib})
        cp.start()
        a2_copies.append(cp)
    for cp in w2_local:
        cp.wait()
    for cp in w2_remote:
        cp.wait_recv()

    spot = (cx, cy)

    def turn(p, by):
        return lax.rem(spot[p] + by + SIDE, SIDE)

    def neighbour(p, by):
        to = turn(p, by)
        return {"head": at(to, cy, core) if p == 0 else at(cx, to, core)}

    def multiply(p, by):
        i = turn(p, by)
        rows = slice(p * half, (p + 1) * half)
        for j in range(SIDE):
            jx, jy = (i, j) if p == 0 else (j, i)
            c[jx, jy, rows, :] = (
                mm(a2[0, rows], w2[jx, jy, 0]) + mm(a2[1, rows], w2[jx, jy, 1])
            ).astype(BF)

    pieces = [(p, n) for n in range(NQ) for p in range(2)]
    index = {u: i for i, u in enumerate(pieces)}
    sends = []

    def part(u, which):
        p, n = u
        start = p * half + n * piece + which * hp
        return slice(start, start + hp)

    def blocks(u, by, which):
        i = turn(u[0], by)
        rows = part(u, which)
        return c.at[i, :, rows, :] if u[0] == 0 else c.at[:, i, rows, :]

    def send1(u, kind, src):
        i = index[u]
        cp = remote(
            src, r1.at[i, kind], s1s.at[i, kind], s1r.at[i, kind], neighbour(u[0], (1, -1)[kind % 2])
        )
        cp.start()
        sends.append(cp)

    def got1(u, kind):
        i = index[u]
        remote(
            r1.at[i, kind], r1.at[i, kind], s1s.at[i, kind], s1r.at[i, kind], neighbour(u[0], 1)
        ).wait_recv()

    def send2(u, kind, src):
        i = index[u]
        cp = remote(
            src, r2.at[i, kind], s2s.at[i, kind], s2r.at[i, kind], neighbour(1 - u[0], (1, -1)[kind % 2])
        )
        cp.start()
        sends.append(cp)

    def got2(u, kind):
        i = index[u]
        remote(
            r2.at[i, kind], r2.at[i, kind], s2s.at[i, kind], s2r.at[i, kind], neighbour(1 - u[0], 1)
        ).wait_recv()

    def forward1(u):
        i = index[u]
        for kind, by, which in ((0, 1, 0), (1, -1, 1)):
            got1(u, kind)
            r1[i, kind] = (
                r1[i, kind].astype(F32) + blocks(u, by, which)[...].astype(F32)
            ).astype(BF)
            send1(u, kind + 4, r1.at[i, kind])

    def finish1(u):
        i = index[u]
        for kind in (2, 3, 4, 5):
            got1(u, kind)
        for which, one, two in ((0, 4, 3), (1, 5, 2)):
            s1[i, :, which * hp : (which + 1) * hp, :] = (
                blocks(u, 0, which)[...].astype(F32) + r1[i, one].astype(F32) + r1[i, two].astype(F32)
            ).astype(BF)
        rows = (slice(0, hp), slice(hp, 2 * hp))
        q = 1 - u[0]
        send2(u, 0, s1.at[i, turn(q, 2), rows[0]])
        send2(u, 1, s1.at[i, turn(q, 2), rows[1]])
        send2(u, 2, s1.at[i, turn(q, 1), rows[1]])
        send2(u, 3, s1.at[i, turn(q, -1), rows[0]])

    def forward2(u):
        i = index[u]
        q = 1 - u[0]
        for kind, by, rows in ((0, 1, slice(0, hp)), (1, -1, slice(hp, 2 * hp))):
            got2(u, kind)
            r2[i, kind] = (
                r2[i, kind].astype(F32) + s1[i, turn(q, by), rows].astype(F32)
            ).astype(BF)
            send2(u, kind + 4, r2.at[i, kind])

    def finish2(u):
        i = index[u]
        for kind in (2, 3, 4, 5):
            got2(u, kind)
        q = 1 - u[0]
        for which, one, two in ((0, 4, 3), (1, 5, 2)):
            rows = part(u, which)
            branch = (
                s1[i, turn(q, 0), which * hp : (which + 1) * hp].astype(F32)
                + r2[i, one].astype(F32)
                + r2[i, two].astype(F32)
            )
            mixed_ref[rows, :] = (xcols[rows, :].astype(F32) + branch).astype(BF)

    for p in range(2):
        a2_copies[p].wait_recv()
        multiply(p, 2)
        send1((p, 0), 0, blocks((p, 0), 2, 0))
        send1((p, 0), 1, blocks((p, 0), 2, 1))
    for p in range(2):
        multiply(p, 1)
        multiply(p, -1)
        send1((p, 0), 2, blocks((p, 0), 1, 1))
        send1((p, 0), 3, blocks((p, 0), -1, 0))
        for n in range(1, NQ):
            send1((p, n), 0, blocks((p, n), 2, 0))
            send1((p, n), 1, blocks((p, n), 2, 1))
    for p in range(2):
        multiply(p, 0)
    x_cols.wait()
    for n in range(NQ):
        for p in range(2):
            forward1((p, n))
            if n > 0:
                send1((p, n), 2, blocks((p, n), 1, 1))
                send1((p, n), 3, blocks((p, n), -1, 0))
        if n > 0:
            for p in range(2):
                finish1((p, n - 1))
            if n > 1:
                for p in range(2):
                    forward2((p, n - 2))
    if NQ > 1:
        for p in range(2):
            forward2((p, NQ - 2))
    for p in range(2):
        finish1((p, NQ - 1))
    for n in range(NQ - 1):
        for p in range(2):
            finish2((p, n))

    r_dev = owners_ref.shape[0]
    eye = lax.broadcasted_iota(jnp.int32, (r_dev, r_dev), 0)
    eye_col = lax.broadcasted_iota(jnp.int32, (r_dev, r_dev), 1)
    same_place = eye == eye_col
    pick = jnp.sum(
        jnp.where(same_place, jnp.broadcast_to(picked_ref[...], (r_dev, r_dev)), 0), axis=1, keepdims=True
    )
    turns = jnp.broadcast_to(turn_ref[...], (r_dev, tokens))
    places = lax.broadcasted_iota(jnp.int32, (r_dev, tokens), 1)
    own_turn = jnp.sum(jnp.where(places == pick, turns, 0), axis=1, keepdims=True)
    member = jnp.where((turns == own_turn) & (places <= pick), 1.0, 0.0)
    count = jnp.sum(member, axis=1, keepdims=True)
    own_col = jnp.broadcast_to(owners_ref[...], (r_dev, r_dev))
    own_row = jnp.sum(jnp.where(same_place, own_col, 0), axis=0, keepdims=True)
    rank = jnp.sum(jnp.where((own_col == own_row) & (eye < eye_col), 1, 0), axis=0, keepdims=True)
    cap = outb.shape[1]
    slot = own_row * cap + rank
    dispatch = jnp.where(
        lax.broadcasted_iota(jnp.int32, (n_head * cap, r_dev), 0) == slot, 1.0, 0.0
    ).astype(BF)

    for p in range(2):
        forward2((p, NQ - 1))
    for p in range(2):
        finish2((p, NQ - 1))

    summary = (mm(member.astype(BF), mixed_ref[...]) / count).astype(BF)
    outb[...] = mm(dispatch, summary).astype(BF).reshape(n_head, cap, col)
    mine = pl.ds(pl.multiple_of(me * col, col), col)
    keep = pltpu.make_async_copy(outb.at[me], inb.at[:, mine], msem.at[2])
    keep.start()

    def hand(i):
        to = lax.rem(me + i, n_head)
        return remote(outb.at[to], inb.at[:, mine], aas.at[i - 1], aar.at[i - 1], {"head": to})

    def hand_out(i, carry):
        hand(i).start()
        return carry

    lax.fori_loop(1, n_head, hand_out, 0)
    cand_load.wait()
    keep.wait()

    def take_in(i, carry):
        hand(i).wait()
        return carry

    lax.fori_loop(1, n_head, take_in, 0)
    scores_ref[...] = mm(inb[...], cand[...], ((1,), (1,)))

    for cp in state_copies + w2_remote + a2_copies + sends:
        cp.wait_send()


def per_device(inputs, w_qkv, w_out, turn_ids, picked, owners, candidates):
    tokens, width = inputs.shape
    n_head = lax.axis_size("head")
    n_seq = lax.axis_size("seq")
    col = width // n_head
    here = w_qkv.shape[2]
    r_dev = picked.shape[1]
    cap = 4 * r_dev // n_head
    nk = width // KB
    units = 2 * NQ
    hp = tokens // (4 * NQ)
    dma = pltpu.SemaphoreType.DMA
    anywhere = pl.BlockSpec(memory_space=pl.ANY)
    vmem = pl.BlockSpec(memory_space=pltpu.VMEM)
    return pl.pallas_call(
        kernel,
        out_shape=(
            jax.ShapeDtypeStruct((tokens, col), BF),
            jax.ShapeDtypeStruct((cap, candidates.shape[0]), F32),
        ),
        in_specs=[anywhere, anywhere, anywhere, vmem, vmem, vmem, anywhere],
        out_specs=(vmem, vmem),
        scratch_shapes=[
            pltpu.VMEM((nk, tokens, KB), BF),
            pltpu.VMEM((3, nk, KB, here), BF),
            pltpu.VMEM((3, tokens, here), F32),
            pltpu.VMEM((3, tokens, here), BF),
            pltpu.VMEM((2, HDIM, HDIM), BF),
            pltpu.VMEM((n_seq - 1, 2, HDIM, HDIM), BF),
            pltpu.VMEM((tokens, here), F32),
            pltpu.VMEM((2, tokens, here), BF),
            pltpu.VMEM((SIDE, SIDE, 2, here, col), BF),
            pltpu.VMEM((SIDE, SIDE, tokens, col), BF),
            pltpu.VMEM((units, 6, SIDE, hp, col), BF),
            pltpu.VMEM((units, SIDE, 2 * hp, col), BF),
            pltpu.VMEM((units, 6, hp, col), BF),
            pltpu.VMEM((tokens, col), BF),
            pltpu.VMEM((n_head, cap, col), BF),
            pltpu.VMEM((cap, width), BF),
            pltpu.VMEM(candidates.shape, BF),
            dma((nk,)),
            dma((3, nk)),
            dma((3,)),
            dma((SIDE * SIDE,)),
            dma((SIDE * SIDE,)),
            dma((SIDE * SIDE,)),
            dma((n_seq - 1,)),
            dma((n_seq - 1,)),
            dma((2,)),
            dma((2,)),
            dma((units, 6)),
            dma((units, 6)),
            dma((units, 6)),
            dma((units, 6)),
            dma((n_head - 1,)),
            dma((n_head - 1,)),
        ],
        compiler_params=pltpu.CompilerParams(
            collective_id=0, has_side_effects=True, vmem_limit_bytes=58 << 20
        ),
    )(inputs, w_qkv, w_out, turn_ids, picked, owners, candidates)


def solution(mesh):
    return jax.shard_map(
        per_device,
        mesh=mesh,
        in_specs=(
            P("seq", None),
            P(None, None, "head"),
            P("head", None),
            P("seq", None),
            P("seq", None),
            P("seq", None),
            P(("seq", "head"), None),
        ),
        out_specs=(P("seq", "head"), P(("seq", "head"), None)),
        check_vma=False,
    )
```

time: 186 us -> 64 us (0.34)
  waiting for transfers between devices: 116 us -> 0 us
  Pallas kernels: 0 us -> 58.9 us
  blocking collectives: 28 us -> 0 us
  matrix products: 25.3 us -> 0 us
  between operations: 14.2 us -> 0.64 us
  local copies, waits for them, and re-layouts: 0.69 us -> 4.3 us
    reduce_scatter x1 -> x0, waiting for transfers between devices: 116 us -> none  [per_device(): lax.psum_scatter(lax.dot_general(w_out, attended, (((0,), (1,)), ((), ())...]
    pallas_call x0 -> x1, Pallas kernels: none -> 58.9 us  [per_device(): pl.pallas_call(kernel, out_shape=(jax.ShapeDtypeStruct((tokens, col), BF)...]
    dot_general x8 -> x0, matrix products: 25.3 us -> none  [the longest x1 12.2 us: per_device(): lax.dot_general(inputs, w_qkv, (((1,), (1,)), ((), ())), preferred_elemen...]
    all_to_all x1 -> x0, blocking collectives: 14.6 us -> none  [per_device(): lax.all_to_all(outgoing, 'head', split_axis=0, concat_axis=0, tiled=True)]
    all_gather x1 -> x0, blocking collectives: 13.4 us -> none  [carried_in(): pieces = lax.all_gather(value, axis)]
    unnamed x10 -> x3, local copies, waits for them, and re-layouts: 0.63 us -> 4.3 us
  transfers between devices with their start and end apart: 1 -> 0, of which waited for: 1 -> 0; matrix products, arithmetic and copies ran while one was open for 0% -> 0% of each run, Pallas kernels for 0% -> 0%
where the time goes in v1:
time: 64 us; the launch traced here: 63.8 us
  Pallas kernels  58.9 us (92%)
  local copies, waits for them, and re-layouts  4.3 us (7%)
  between operations  0.64 us (1%)
    pallas_call x1, Pallas kernels, per_device(): pl.pallas_call(kernel, out_shape=(jax.ShapeDtypeStruct((tokens, col), BF)...  58.9 us
    unnamed x3, local copies, waits for them, and re-layouts  4.3 us

profile of v1, /device:TPU:1, one launch (start us, length us, event | category | flops | bytes accessed | tf_op | source)
XLA Modules:
  0.0 63.8 jit_solution(689882795503571224)
XLA Ops:
  0.6 1.4 %copy.9.owners_ref = s32[64,1]{1,0:T(8,128)} copy(s32[64,1]{0,1:T(1,128)} %param.12) | data formatting | bytes 512 | tf_op args[5]
  2.0 58.9 %shard_map.86 = (bf16[512,256]{1,0:T(8,128)(2,1)}, f32[8,64]{1,0:T(8,128)}) custom-call(bf16[512,8192]{1,0:T(8,128)(2,1)} %x_hbm.1, bf16[3,8192,256]{2,1,0:T(8,128)(2,1)} %wqkv_hbm.1, bf16[256,8192]{1,0:T(8,128)(2,1)} %wout_hbm.1, s32[1,512]{1,0:T(1,128)} %turn_ref.1, s32[1,64]{1,0:T(1,128)} %picked_ref.1, s32[64,1]{1,0:T(8,128)} %copy.9.owners_ref, ...), custom_call_target="tpu_custom_call" | custom-call | tf_op jit(solution)/shard_map/pallas_call | solution.py:403
  60.8 1.7 %copy.12 = bf16[512,256]{1,0:T(8,128)(2,1)} copy(bf16[512,256]{1,0:T(8,128)(2,1)} %get-tuple-element.4) | data formatting | bytes 524288
  62.5 1.3 %copy.13 = f32[8,64]{1,0:T(8,128)} copy(f32[8,64]{1,0:T(8,128)} %get-tuple-element.5) | data formatting | bytes 4096

commit v2 on v1

--- a/solution.py
+++ b/solution.py
@@ -11,6 +11,7 @@
 SIDE = 4
 KB = 1024
 AHEAD = 4
+MEET = 4
 NQ = 2
 MESH = pl.DeviceIdType.MESH
 BF = jnp.bfloat16
@@ -22,17 +23,17 @@
 
 
 def kernel(
-    x_hbm, wqkv_hbm, wout_hbm, turn_ref, picked_ref, owners_ref, cand_hbm,
+    x_hbm, wqkv_hbm, wout_hbm, turn_hbm, picked_hbm, owners_hbm, cand_hbm,
     mixed_ref, scores_ref,
-    xbuf, wbuf, acc, qkv, st, st_in, pre, a2, w2, c, r1, s1, r2, xcols, outb, inb, cand,
-    xsem, wsem, msem, w2l, w2s, w2r, sts, strr, a2s, a2r, s1s, s1r, s2s, s2r, aas, aar,
+    xbuf, wbuf, acc, qkv, st, st_in, pre, a2, w2, c, r1, s1, r2, xcols, outb, inb, cand, turn_ref, picked_ref, owners_ref,
+    xsem, wsem, qsem, msem, w2l, w2s, w2r, sts, strr, a2s, a2r, s1s, s1r, s2s, s2r, aas, aar,
 ):
     tokens, col = xcols.shape
     nk = xbuf.shape[0]
     n_head = outb.shape[0]
     n_seq = st_in.shape[0] + 1
-    half = tokens // 2
-    piece = half // NQ
+    block = tokens // NQ
+    piece = block // 2
     hp = piece // 2
     z = lax.axis_index("seq")
     me = lax.axis_index("head")
@@ -50,10 +51,15 @@
             x_hbm.at[:, pl.ds(pl.multiple_of(k * KB, KB), KB)], xbuf.at[k], xsem.at[k]
         )
 
-    def w_load(n, k):
+    def kv_load(k):
+        rows = pl.ds(pl.multiple_of(k * KB, KB), KB)
         return pltpu.make_async_copy(
-            wqkv_hbm.at[n, pl.ds(pl.multiple_of(k * KB, KB), KB), :], wbuf.at[n, k], wsem.at[n, k]
-        )
+            wqkv_hbm.at[pl.ds(1, 2), rows, :], wbuf.at[k, pl.ds(1, 2)], wsem.at[k]
+        )
+
+    def q_load(k):
+        rows = pl.ds(pl.multiple_of(k * KB, KB), KB)
+        return pltpu.make_async_copy(wqkv_hbm.at[0, rows, :], wbuf.at[k, 0], qsem.at[k])
 
     def remote(src, dst, ssem, rsem, to):
         return pltpu.make_async_remote_copy(
@@ -61,9 +67,8 @@
         )
 
     for k in range(AHEAD):
+        kv_load(k).start()
         x_load(k).start()
-        w_load(1, k).start()
-        w_load(2, k).start()
 
     barrier = pltpu.get_barrier_semaphore()
 
@@ -83,28 +88,42 @@
 
     def kv_step(k, carry):
         x_load(k).wait()
-        w_load(1, k).wait()
-        w_load(2, k).wait()
+        kv_load(k).wait()
 
         @pl.when(k + AHEAD < nk)
         def _():
+            kv_load(k + AHEAD).start()
             x_load(k + AHEAD).start()
-            w_load(1, k + AHEAD).start()
-            w_load(2, k + AHEAD).start()
 
         @pl.when(k + AHEAD >= nk)
         def _():
-            w_load(0, k + AHEAD - nk).start()
-
-        acc[1] += mm(xbuf[k], wbuf[1, k])
-        acc[2] += mm(xbuf[k], wbuf[2, k])
+            q_load(k + AHEAD - nk).start()
+
+        acc[1] += mm(xbuf[k], wbuf[k, 1])
+        acc[2] += mm(xbuf[k], wbuf[k, 2])
         return carry
 
-    lax.fori_loop(0, nk, kv_step, 0)
+    lax.fori_loop(0, MEET, kv_step, 0)
+
+    pl.semaphore_wait(barrier, n_head - 1 + n_seq - 1)
+
+    w2_local, w2_remote = [], []
+    for j in range(SIDE * SIDE):
+        jx, jy = j // SIDE, j % SIDE
+        mine = pl.ds(pl.multiple_of((2 * j + core) * col, col), col)
+        theirs = pl.ds(pl.multiple_of((2 * j + 1 - core) * col, col), col)
+        w2_local.append(
+            pltpu.make_async_copy(wout_hbm.at[:, mine], w2.at[jx, jy, core], w2l.at[j])
+        )
+        w2_remote.append(
+            remote(wout_hbm.at[:, theirs], w2.at[jx, jy, core], w2s.at[j], w2r.at[j], {"head": sib})
+        )
+    for cp in w2_local + w2_remote:
+        cp.start()
+
+    lax.fori_loop(MEET, nk, kv_step, 0)
     qkv[1] = acc[1].astype(BF)
     qkv[2] = acc[2].astype(BF)
-
-    pl.semaphore_wait(barrier, n_head - 1 + n_seq - 1)
 
     for h in range(2):
         hs = slice(h * HDIM, (h + 1) * HDIM)
@@ -116,45 +135,40 @@
     for cp in state_copies:
         cp.start()
 
-    w2_local, w2_remote = [], []
-    for j in range(SIDE * SIDE):
-        jx, jy = j // SIDE, j % SIDE
-        mine = pl.ds(pl.multiple_of((2 * j + core) * col, col), col)
-        theirs = pl.ds(pl.multiple_of((2 * j + 1 - core) * col, col), col)
-        w2_local.append(
-            pltpu.make_async_copy(wout_hbm.at[:, mine], w2.at[jx, jy, core], w2l.at[j])
-        )
-        w2_remote.append(
-            remote(wout_hbm.at[:, theirs], w2.at[jx, jy, core], w2s.at[j], w2r.at[j], {"head": sib})
-        )
-    for cp in w2_local + w2_remote:
-        cp.start()
     x_cols = pltpu.make_async_copy(
         x_hbm.at[:, pl.ds(pl.multiple_of(me * col, col), col)], xcols, msem.at[0]
     )
     x_cols.start()
     cand_load = pltpu.make_async_copy(cand_hbm, cand, msem.at[1])
     cand_load.start()
+    small_loads = [
+        pltpu.make_async_copy(src, dst, msem.at[3 + i])
+        for i, (src, dst) in enumerate(
+            ((turn_hbm, turn_ref), (picked_hbm, picked_ref), (owners_hbm, owners_ref))
+        )
+    ]
+    for cp in small_loads:
+        cp.start()
 
     def q_step(k, carry):
-        w_load(0, k).wait()
+        q_load(k).wait()
 
         @pl.when(k + AHEAD < nk)
         def _():
-            w_load(0, k + AHEAD).start()
-
-        acc[0] += mm(xbuf[k], wbuf[0, k])
+            q_load(k + AHEAD).start()
+
+        acc[0] += mm(xbuf[k], wbuf[k, 0])
         return carry
 
     lax.fori_loop(0, nk, q_step, 0)
     qkv[0] = acc[0].astype(BF)
 
-    for b in range(2):
-        rows = slice(b * half, (b + 1) * half)
-        seen = (b + 1) * half
+    def local(b):
+        rows = slice(b * block, (b + 1) * block)
+        seen = (b + 1) * block
         ok = (
-            lax.broadcasted_iota(jnp.int32, (half, seen), 0) + b * half
-            >= lax.broadcasted_iota(jnp.int32, (half, seen), 1)
+            lax.broadcasted_iota(jnp.int32, (block, seen), 0) + b * block
+            >= lax.broadcasted_iota(jnp.int32, (block, seen), 1)
         )
         for h in range(2):
             hs = slice(h * HDIM, (h + 1) * HDIM)
@@ -162,6 +176,18 @@
             sc = jnp.where(ok, sc, 0.0).astype(BF)
             pre[rows, hs] = mm(sc, qkv[2, :seen, hs])
 
+    def attend(b, prefix):
+        rows = slice(b * block, (b + 1) * block)
+        for h in range(2):
+            hs = slice(h * HDIM, (h + 1) * HDIM)
+            summed = pre[rows, hs] + mm(qkv[0, rows, hs], prefix[h])
+            normed = summed * lax.rsqrt(jnp.mean(summed * summed, axis=-1, keepdims=True) + 1e-05)
+            a2[core, rows, hs] = normed.astype(BF)
+        cp = remote(a2.at[core, rows], a2.at[core, rows], a2s.at[b], a2r.at[b], {"head": sib})
+        cp.start()
+        return cp
+
+    local(0)
     for cp in state_copies:
         cp.wait_recv()
     prefix = []
@@ -170,17 +196,10 @@
         for d in range(1, n_seq):
             total = total + jnp.where(z >= d, st_in[d - 1, h].astype(F32), 0.0)
         prefix.append(total.astype(BF))
-    a2_copies = []
-    for b in range(2):
-        rows = slice(b * half, (b + 1) * half)
-        for h in range(2):
-            hs = slice(h * HDIM, (h + 1) * HDIM)
-            summed = pre[rows, hs] + mm(qkv[0, rows, hs], prefix[h])
-            normed = summed * lax.rsqrt(jnp.mean(summed * summed, axis=-1, keepdims=True) + 1e-05)
-            a2[core, rows, hs] = normed.astype(BF)
-        cp = remote(a2.at[core, rows], a2.at[core, rows], a2s.at[b], a2r.at[b], {"head": sib})
-        cp.start()
-        a2_copies.append(cp)
+    a2_copies = [attend(0, prefix)]
+    for b in range(1, NQ):
+        local(b)
+        a2_copies.append(attend(b, prefix))
     for cp in w2_local:
         cp.wait()
     for cp in w2_remote:
@@ -195,11 +214,10 @@
         to = turn(p, by)
         return {"head": at(to, cy, core) if p == 0 else at(cx, to, core)}
 
-    def multiply(p, by):
-        i = turn(p, by)
-        rows = slice(p * half, (p + 1) * half)
-        for j in range(SIDE):
-            jx, jy = (i, j) if p == 0 else (j, i)
+    def multiply(n, places):
+        rows = slice(n * block, (n + 1) * block)
+        for bx, by in places:
+            jx, jy = turn(0, bx), turn(1, by)
             c[jx, jy, rows, :] = (
                 mm(a2[0, rows], w2[jx, jy, 0]) + mm(a2[1, rows], w2[jx, jy, 1])
             ).astype(BF)
@@ -210,7 +228,7 @@
 
     def part(u, which):
         p, n = u
-        start = p * half + n * piece + which * hp
+        start = n * block + p * piece + which * hp
         return slice(start, start + hp)
 
     def blocks(u, by, which):
@@ -294,44 +312,41 @@
             )
             mixed_ref[rows, :] = (xcols[rows, :].astype(F32) + branch).astype(BF)
 
-    for p in range(2):
-        a2_copies[p].wait_recv()
-        multiply(p, 2)
-        send1((p, 0), 0, blocks((p, 0), 2, 0))
-        send1((p, 0), 1, blocks((p, 0), 2, 1))
-    for p in range(2):
-        multiply(p, 1)
-        multiply(p, -1)
-        send1((p, 0), 2, blocks((p, 0), 1, 1))
-        send1((p, 0), 3, blocks((p, 0), -1, 0))
-        for n in range(1, NQ):
+    steps = (2, 1, -1, 0)
+    first = [(2, b) for b in steps] + [(b, 2) for b in steps[1:]]
+    second = [(a, b) for a in steps[1:] for b in steps[1:] if (a, b) != (0, 0)]
+
+    for n in range(NQ):
+        a2_copies[n].wait_recv()
+        multiply(n, first)
+        for p in range(2):
             send1((p, n), 0, blocks((p, n), 2, 0))
             send1((p, n), 1, blocks((p, n), 2, 1))
-    for p in range(2):
-        multiply(p, 0)
-    x_cols.wait()
-    for n in range(NQ):
-        for p in range(2):
-            forward1((p, n))
-            if n > 0:
-                send1((p, n), 2, blocks((p, n), 1, 1))
-                send1((p, n), 3, blocks((p, n), -1, 0))
         if n > 0:
             for p in range(2):
-                finish1((p, n - 1))
-            if n > 1:
-                for p in range(2):
-                    forward2((p, n - 2))
-    if NQ > 1:
+                forward1((p, n - 1))
+        multiply(n, second)
         for p in range(2):
-            forward2((p, NQ - 2))
+            send1((p, n), 2, blocks((p, n), 1, 1))
+            send1((p, n), 3, blocks((p, n), -1, 0))
+        multiply(n, [(0, 0)])
+    x_cols.wait()
+    for p in range(2):
+        forward1((p, NQ - 1))
+    for n in range(NQ - 1):
+        for p in range(2):
+            finish1((p, n))
+        for p in range(2):
+            forward2((p, n))
     for p in range(2):
         finish1((p, NQ - 1))
     for n in range(NQ - 1):
         for p in range(2):
             finish2((p, n))
 
-    r_dev = owners_ref.shape[0]
+    for cp in small_loads:
+        cp.wait()
+    r_dev = owners_ref.shape[1]
     eye = lax.broadcasted_iota(jnp.int32, (r_dev, r_dev), 0)
     eye_col = lax.broadcasted_iota(jnp.int32, (r_dev, r_dev), 1)
     same_place = eye == eye_col
@@ -343,8 +358,10 @@
     own_turn = jnp.sum(jnp.where(places == pick, turns, 0), axis=1, keepdims=True)
     member = jnp.where((turns == own_turn) & (places <= pick), 1.0, 0.0)
     count = jnp.sum(member, axis=1, keepdims=True)
-    own_col = jnp.broadcast_to(owners_ref[...], (r_dev, r_dev))
-    own_row = jnp.sum(jnp.where(same_place, own_col, 0), axis=0, keepdims=True)
+    own_row = owners_ref[...]
+    own_col = jnp.sum(
+        jnp.where(same_place, jnp.broadcast_to(own_row, (r_dev, r_dev)), 0), axis=1, keepdims=True
+    )
     rank = jnp.sum(jnp.where((own_col == own_row) & (eye < eye_col), 1, 0), axis=0, keepdims=True)
     cap = outb.shape[1]
     slot = own_row * cap + rank
@@ -384,6 +401,17 @@
 
     for cp in state_copies + w2_remote + a2_copies + sends:
         cp.wait_send()
+
+
+def hand_over(mixed_in, scores_in, mixed_out, scores_out, sem):
+    copies = [
+        pltpu.make_async_copy(mixed_in, mixed_out, sem.at[0]),
+        pltpu.make_async_copy(scores_in, scores_out, sem.at[1]),
+    ]
+    for cp in copies:
+        cp.start()
+    for cp in copies:
+        cp.wait()
 
 
 def per_device(inputs, w_qkv, w_out, turn_ids, picked, owners, candidates):
@@ -398,19 +426,19 @@
     units = 2 * NQ
     hp = tokens // (4 * NQ)
     dma = pltpu.SemaphoreType.DMA
-    anywhere = pl.BlockSpec(memory_space=pl.ANY)
+    hbm = pl.BlockSpec(memory_space=pltpu.HBM)
     vmem = pl.BlockSpec(memory_space=pltpu.VMEM)
-    return pl.pallas_call(
+    results = pl.pallas_call(
         kernel,
         out_shape=(
             jax.ShapeDtypeStruct((tokens, col), BF),
             jax.ShapeDtypeStruct((cap, candidates.shape[0]), F32),
         ),
-        in_specs=[anywhere, anywhere, anywhere, vmem, vmem, vmem, anywhere],
+        in_specs=[hbm] * 7,
         out_specs=(vmem, vmem),
         scratch_shapes=[
             pltpu.VMEM((nk, tokens, KB), BF),
-            pltpu.VMEM((3, nk, KB, here), BF),
+            pltpu.VMEM((nk, 3, KB, here), BF),
             pltpu.VMEM((3, tokens, here), F32),
             pltpu.VMEM((3, tokens, here), BF),
             pltpu.VMEM((2, HDIM, HDIM), BF),
@@ -426,16 +454,20 @@
             pltpu.VMEM((n_head, cap, col), BF),
             pltpu.VMEM((cap, width), BF),
             pltpu.VMEM(candidates.shape, BF),
+            pltpu.VMEM(turn_ids.shape, jnp.int32),
+            pltpu.VMEM(picked.shape, jnp.int32),
+            pltpu.VMEM((1, r_dev), jnp.int32),
             dma((nk,)),
-            dma((3, nk)),
-            dma((3,)),
+            dma((nk,)),
+            dma((nk,)),
+            dma((6,)),
             dma((SIDE * SIDE,)),
             dma((SIDE * SIDE,)),
             dma((SIDE * SIDE,)),
             dma((n_seq - 1,)),
             dma((n_seq - 1,)),
-            dma((2,)),
-            dma((2,)),
+            dma((NQ,)),
+            dma((NQ,)),
             dma((units, 6)),
             dma((units, 6)),
             dma((units, 6)),
@@ -444,9 +476,25 @@
             dma((n_head - 1,)),
         ],
         compiler_params=pltpu.CompilerParams(
-            collective_id=0, has_side_effects=True, vmem_limit_bytes=58 << 20
+            collective_id=0, has_side_effects=True, vmem_limit_bytes=53 << 20
         ),
-    )(inputs, w_qkv, w_out, turn_ids, picked, owners, candidates)
+    )(
+        inputs,
+        w_qkv,
+        w_out,
+        pltpu.with_memory_space_constraint(turn_ids, pltpu.HBM),
+        pltpu.with_memory_space_constraint(picked, pltpu.HBM),
+        pltpu.with_memory_space_constraint(owners.reshape(1, r_dev), pltpu.HBM),
+        candidates,
+    )
+    return pl.pallas_call(
+        hand_over,
+        out_shape=tuple(jax.ShapeDtypeStruct(a.shape, a.dtype) for a in results),
+        in_specs=[pl.BlockSpec(memory_space=pltpu.VMEM)] * 2,
+        out_specs=(pl.BlockSpec(memory_space=pltpu.HBM),) * 2,
+        scratch_shapes=[dma((2,))],
+        compiler_params=pltpu.CompilerParams(vmem_limit_bytes=4 << 20),
+    )(*results)
 
 
 def solution(mesh):

time: 64 us -> 58.9 us (0.920)
  local copies, waits for them, and re-layouts: 4.3 us -> 0 us
  Pallas kernels: 58.9 us -> 58.2 us
    unnamed x3 -> x0, local copies, waits for them, and re-layouts: 4.3 us -> none
    pallas_call x1, Pallas kernels: 58.9 us -> 57.4 us  [per_device(): pl.pallas_call(kernel, out_shape=(jax.ShapeDtypeStruct((tokens, col), BF)...]
    pallas_call x0 -> x1, Pallas kernels: none -> 0.72 us  [per_device(): pl.pallas_call(hand_over, out_shape=tuple((jax.ShapeDtypeStruct(a.shape,...]
where the time goes in v2:
time: 58.9 us; the launch traced here: 58.8 us
  Pallas kernels  58.2 us (99%)
  between operations  0.64 us (1%)
    pallas_call x1, Pallas kernels, per_device(): pl.pallas_call(kernel, out_shape=(jax.ShapeDtypeStruct((tokens, col), BF)...  57.4 us

profile of v2, /device:TPU:1, one launch (start us, length us, event | category | flops | bytes accessed | tf_op | source)
XLA Modules:
  0.0 58.8 jit_solution(5418096116589627628)
XLA Ops:
  0.6 57.4 %shard_map.86 = (bf16[512,256]{1,0:T(8,128)(2,1)S(1)}, f32[8,64]{1,0:T(8,128)S(1)}) custom-call(bf16[512,8192]{1,0:T(8,128)(2,1)} %x_hbm.1, bf16[3,8192,256]{2,1,0:T(8,128)(2,1)} %wqkv_hbm.1, bf16[256,8192]{1,0:T(8,128)(2,1)} %wout_hbm.1, s32[1,512]{1,0:T(1,128)} %turn_hbm.1, s32[1,64]{1,0:T(1,128)} %picked_hbm.1, s32[1,64]{1,0:T(1,128)} %bitcast.1, ...), custom_call_target="tpu_custom_call" | custom-call | tf_op jit(solution)/shard_map/pallas_call | solution.py:431
  58.1 0.7 %shard_map.87 = (bf16[512,256]{1,0:T(8,128)(2,1)}, f32[8,64]{1,0:T(8,128)}) custom-call(bf16[512,256]{1,0:T(8,128)(2,1)S(1)} %get-tuple-element.4.mixed_in, f32[8,64]{1,0:T(8,128)S(1)} %get-tuple-element.5.scores_in), custom_call_target="tpu_custom_call" | custom-call | tf_op jit(solution)/shard_map/pallas_call | solution.py:490

commit v3 on v2

--- a/solution.py
+++ b/solution.py
@@ -9,9 +9,9 @@
 
 HDIM = 128
 SIDE = 4
-KB = 1024
-AHEAD = 4
-MEET = 4
+KB = 2048
+AHEAD = 2
+MEET = 2
 NQ = 2
 MESH = pl.DeviceIdType.MESH
 BF = jnp.bfloat16
@@ -25,7 +25,7 @@
 def kernel(
     x_hbm, wqkv_hbm, wout_hbm, turn_hbm, picked_hbm, owners_hbm, cand_hbm,
     mixed_ref, scores_ref,
-    xbuf, wbuf, acc, qkv, st, st_in, pre, a2, w2, c, r1, s1, r2, xcols, outb, inb, cand, turn_ref, picked_ref, owners_ref,
+    xbuf, wbuf, acc, qkv, st, st_in, carried, pre, a2, w2, c, r1, s1, r2, xcols, outb, inb, cand, turn_ref, picked_ref, owners_ref,
     xsem, wsem, qsem, msem, w2l, w2s, w2r, sts, strr, a2s, a2r, s1s, s1r, s2s, s2r, aas, aar,
 ):
     tokens, col = xcols.shape
@@ -125,15 +125,19 @@
     qkv[1] = acc[1].astype(BF)
     qkv[2] = acc[2].astype(BF)
 
+    def state_copy(d, h):
+        i = 2 * (d - 1) + h
+        to = {"seq": lax.rem(z + d, n_seq)}
+        return remote(st.at[h], st_in.at[d - 1, h], sts.at[i], strr.at[i], to)
+
     for h in range(2):
         hs = slice(h * HDIM, (h + 1) * HDIM)
         st[h] = mm(qkv[1, :, hs], qkv[2, :, hs], ((0,), (0,))).astype(BF)
-    state_copies = [
-        remote(st, st_in.at[d - 1], sts.at[d - 1], strr.at[d - 1], {"seq": lax.rem(z + d, n_seq)})
-        for d in range(1, n_seq)
-    ]
-    for cp in state_copies:
-        cp.start()
+        for d in range(1, n_seq):
+
+            @pl.when(z + d < n_seq)
+            def _():
+                state_copy(d, h).start()
 
     x_cols = pltpu.make_async_copy(
         x_hbm.at[:, pl.ds(pl.multiple_of(me * col, col), col)], xcols, msem.at[0]
@@ -188,14 +192,16 @@
         return cp
 
     local(0)
-    for cp in state_copies:
-        cp.wait_recv()
-    prefix = []
-    for h in range(2):
-        total = jnp.zeros((HDIM, HDIM), F32)
-        for d in range(1, n_seq):
-            total = total + jnp.where(z >= d, st_in[d - 1, h].astype(F32), 0.0)
-        prefix.append(total.astype(BF))
+    carried[...] = jnp.zeros_like(carried)
+    for d in range(1, n_seq):
+
+        @pl.when(z >= d)
+        def _():
+            for h in range(2):
+                state_copy(d, h).wait_recv()
+                carried[h] += st_in[d - 1, h].astype(F32)
+
+    prefix = [carried[h].astype(BF) for h in range(2)]
     a2_copies = [attend(0, prefix)]
     for b in range(1, NQ):
         local(b)
@@ -399,7 +405,14 @@
     lax.fori_loop(1, n_head, take_in, 0)
     scores_ref[...] = mm(inb[...], cand[...], ((1,), (1,)))
 
-    for cp in state_copies + w2_remote + a2_copies + sends:
+    for d in range(1, n_seq):
+
+        @pl.when(z + d < n_seq)
+        def _():
+            for h in range(2):
+                state_copy(d, h).wait_send()
+
+    for cp in w2_remote + a2_copies + sends:
         cp.wait_send()
 
 
@@ -443,6 +456,7 @@
             pltpu.VMEM((3, tokens, here), BF),
             pltpu.VMEM((2, HDIM, HDIM), BF),
             pltpu.VMEM((n_seq - 1, 2, HDIM, HDIM), BF),
+            pltpu.VMEM((2, HDIM, HDIM), F32),
             pltpu.VMEM((tokens, here), F32),
             pltpu.VMEM((2, tokens, here), BF),
             pltpu.VMEM((SIDE, SIDE, 2, here, col), BF),
@@ -464,8 +478,8 @@
             dma((SIDE * SIDE,)),
             dma((SIDE * SIDE,)),
             dma((SIDE * SIDE,)),
-            dma((n_seq - 1,)),
-            dma((n_seq - 1,)),
+            dma((2 * n_seq - 2,)),
+            dma((2 * n_seq - 2,)),
             dma((NQ,)),
             dma((NQ,)),
             dma((units, 6)),

time: 58.9 us -> 55.2 us (0.937)
  Pallas kernels: 58.2 us -> 54.5 us
    pallas_call x1, Pallas kernels: 57.4 us -> 53.7 us  [per_device(): pl.pallas_call(kernel, out_shape=(jax.ShapeDtypeStruct((tokens, col), BF)...]
where the time goes in v3:
time: 55.2 us; the launch traced here: 55.1 us
  Pallas kernels  54.5 us (99%)
  between operations  0.64 us (1%)
    pallas_call x1, Pallas kernels, per_device(): pl.pallas_call(kernel, out_shape=(jax.ShapeDtypeStruct((tokens, col), BF)...  53.7 us

profile of v3, /device:TPU:1, one launch (start us, length us, event | category | flops | bytes accessed | tf_op | source)
XLA Modules:
  0.0 55.1 jit_solution(7177149960933962502)
XLA Ops:
  0.6 53.7 %shard_map.86 = (bf16[512,256]{1,0:T(8,128)(2,1)S(1)}, f32[8,64]{1,0:T(8,128)S(1)}) custom-call(bf16[512,8192]{1,0:T(8,128)(2,1)} %x_hbm.1, bf16[3,8192,256]{2,1,0:T(8,128)(2,1)} %wqkv_hbm.1, bf16[256,8192]{1,0:T(8,128)(2,1)} %wout_hbm.1, s32[1,512]{1,0:T(1,128)} %turn_hbm.1, s32[1,64]{1,0:T(1,128)} %picked_hbm.1, s32[1,64]{1,0:T(1,128)} %bitcast.1, ...), custom_call_target="tpu_custom_call" | custom-call | tf_op jit(solution)/shard_map/pallas_call | solution.py:444
  54.4 0.7 %shard_map.87 = (bf16[512,256]{1,0:T(8,128)(2,1)}, f32[8,64]{1,0:T(8,128)}) custom-call(bf16[512,256]{1,0:T(8,128)(2,1)S(1)} %get-tuple-element.4.mixed_in, f32[8,64]{1,0:T(8,128)S(1)} %get-tuple-element.5.scores_in), custom_call_target="tpu_custom_call" | custom-call | tf_op jit(solution)/shard_map/pallas_call | solution.py:504

commit v4 on v3

--- a/solution.py
+++ b/solution.py
@@ -10,8 +10,8 @@
 HDIM = 128
 SIDE = 4
 KB = 2048
-AHEAD = 2
-MEET = 2
+AHEAD = 4
+MEET = 3
 NQ = 2
 MESH = pl.DeviceIdType.MESH
 BF = jnp.bfloat16

time: 55.2 us -> 55.1 us (level)
  no operation moved by 1% of the time
where the time goes in v4:
time: 55.1 us; the launch traced here: 55 us
  Pallas kernels  54.4 us (99%)
  between operations  0.64 us (1%)
    pallas_call x1, Pallas kernels, per_device(): pl.pallas_call(kernel, out_shape=(jax.ShapeDtypeStruct((tokens, col), BF)...  53.6 us

profile of v4, /device:TPU:1, one launch (start us, length us, event | category | flops | bytes accessed | tf_op | source)
XLA Modules:
  0.0 55.0 jit_solution(10662496648779572875)
XLA Ops:
  0.6 53.6 %shard_map.86 = (bf16[512,256]{1,0:T(8,128)(2,1)S(1)}, f32[8,64]{1,0:T(8,128)S(1)}) custom-call(bf16[512,8192]{1,0:T(8,128)(2,1)} %x_hbm.1, bf16[3,8192,256]{2,1,0:T(8,128)(2,1)} %wqkv_hbm.1, bf16[256,8192]{1,0:T(8,128)(2,1)} %wout_hbm.1, s32[1,512]{1,0:T(1,128)} %turn_hbm.1, s32[1,64]{1,0:T(1,128)} %picked_hbm.1, s32[1,64]{1,0:T(1,128)} %bitcast.1, ...), custom_call_target="tpu_custom_call" | custom-call | tf_op jit(solution)/shard_map/pallas_call | solution.py:444
  54.3 0.7 %shard_map.87 = (bf16[512,256]{1,0:T(8,128)(2,1)}, f32[8,64]{1,0:T(8,128)}) custom-call(bf16[512,256]{1,0:T(8,128)(2,1)S(1)} %get-tuple-element.4.mixed_in, f32[8,64]{1,0:T(8,128)S(1)} %get-tuple-element.5.scores_in), custom_call_target="tpu_custom_call" | custom-call | tf_op jit(solution)/shard_map/pallas_call | solution.py:504

commit v5 on v4

--- a/solution.py
+++ b/solution.py
@@ -222,11 +222,11 @@
 
     def multiply(n, places):
         rows = slice(n * block, (n + 1) * block)
+        left = jnp.concatenate([a2[0, rows], a2[1, rows]], axis=1)
         for bx, by in places:
             jx, jy = turn(0, bx), turn(1, by)
-            c[jx, jy, rows, :] = (
-                mm(a2[0, rows], w2[jx, jy, 0]) + mm(a2[1, rows], w2[jx, jy, 1])
-            ).astype(BF)
+            right = w2[jx, jy].reshape(left.shape[1], col)
+            c[jx, jy, rows, :] = mm(left, right).astype(BF)
 
     pieces = [(p, n) for n in range(NQ) for p in range(2)]
     index = {u: i for i, u in enumerate(pieces)}

time: 55.1 us -> 55.1 us (level)
  no operation moved by 1% of the time
where the time goes in v5:
time: 55.1 us; the launch traced here: 55 us
  Pallas kernels  54.4 us (99%)
  between operations  0.64 us (1%)
    pallas_call x1, Pallas kernels, per_device(): pl.pallas_call(kernel, out_shape=(jax.ShapeDtypeStruct((tokens, col), BF)...  53.6 us

profile of v5, /device:TPU:1, one launch (start us, length us, event | category | flops | bytes accessed | tf_op | source)
XLA Modules:
  0.0 55.0 jit_solution(17562232828787029276)
XLA Ops:
  0.6 53.6 %shard_map.86 = (bf16[512,256]{1,0:T(8,128)(2,1)S(1)}, f32[8,64]{1,0:T(8,128)S(1)}) custom-call(bf16[512,8192]{1,0:T(8,128)(2,1)} %x_hbm.1, bf16[3,8192,256]{2,1,0:T(8,128)(2,1)} %wqkv_hbm.1, bf16[256,8192]{1,0:T(8,128)(2,1)} %wout_hbm.1, s32[1,512]{1,0:T(1,128)} %turn_hbm.1, s32[1,64]{1,0:T(1,128)} %picked_hbm.1, s32[1,64]{1,0:T(1,128)} %bitcast.1, ...), custom_call_target="tpu_custom_call" | custom-call | tf_op jit(solution)/shard_map/pallas_call | solution.py:444
  54.3 0.7 %shard_map.87 = (bf16[512,256]{1,0:T(8,128)(2,1)}, f32[8,64]{1,0:T(8,128)}) custom-call(bf16[512,256]{1,0:T(8,128)(2,1)S(1)} %get-tuple-element.4.mixed_in, f32[8,64]{1,0:T(8,128)S(1)} %get-tuple-element.5.scores_in), custom_call_target="tpu_custom_call" | custom-call | tf_op jit(solution)/shard_map/pallas_call | solution.py:504
